TPU v7x, 256 devices: a whole 4x4x8 slice. The times are simulated.
256 devices in a mesh: tok: 32 (over z, x), hid: 8 (over y, core).
Axes of the slice: x: 4, y: 4, z: 8, core: 2. Of those that a mesh axis runs over, the one named last changes fastest.
Arguments:
- inputs: float32 [4096, 4096], P('tok'), may hold values from -6 to 6
- cotangent: float32 [4096, 4096], P('tok'), may hold values from -6 to 6
- up_blocks: float32 [112, 4, 128, 128], P('hid', None, 'tok'), may hold values from -0.25 to 0.25
- down_blocks: float32 [112, 4, 128, 128], P('hid', None, 'tok'), may hold values from -0.25 to 0.25
- up_index: int32 [112, 4], P('hid'), may hold values from 0 to 31, all different within a row
- down_index: int32 [112, 4], P('hid'), may hold values from 0 to 31, all different within a row
- mom_up: float32 [112, 4, 128, 128], P('hid', None, 'tok'), may hold values from -6 to 6
- mom_down: float32 [112, 4, 128, 128], P('hid', None, 'tok'), may hold values from -6 to 6
Outputs:
- input_grad: float32 [4096, 4096], P('tok', 'hid')
- new_mom_up: float32 [112, 4, 128, 128], P('hid', None, 'tok')
- new_mom_down: float32 [112, 4, 128, 128], P('hid', None, 'tok')
Inputs may be any that keep to these rules, and one draw needn't show every extreme that they name: `up_index`: each row lists 4 different model blocks, and every model block appears in some row. `down_index`: each row lists 4 different model blocks, and every model block appears in some row.
All inputs are finite; a program needn't handle non-finite values.
Results may differ from a plain program's by a relative error of at most 0.0003.
Values sent between devices are 32-bit elements; how exact they have to be, the bound alone decides.
A program may use at most 64 MiB of HBM per device.

v0:
```python
import jax
import jax.numpy as jnp
from jax import lax
from jax.sharding import PartitionSpec as P


def shards(inputs, cotangent, up_blocks, down_blocks, up_index, down_index, mom_up, mom_down):
    highest = lax.Precision.HIGHEST
    row_count = inputs.shape[0]
    block = up_blocks.shape[3]
    block_count = inputs.shape[1] // block
    up_full, down_full = (
        lax.all_gather(up_blocks, "tok", axis=2, tiled=True),
        lax.all_gather(down_blocks, "tok", axis=2, tiled=True),
    )
    grad_scale = (row_count * lax.axis_size("tok")) ** (-0.5)
    x_blocks = inputs.reshape(row_count, block_count, block)
    cot_blocks = cotangent.reshape(row_count, block_count, block)
    x_sel = jnp.take(x_blocks, up_index, axis=1)
    cot_sel = jnp.take(cot_blocks, down_index, axis=1)
    pre_act = jnp.einsum("rfkd,fkdc->rfc", x_sel, up_full, precision=highest)
    sigmoid_pre = jax.nn.sigmoid(pre_act)
    activation = pre_act * sigmoid_pre
    grad_act = jnp.einsum("rfkd,fkcd->rfc", cot_sel, down_full, precision=highest)
    grad_pre = grad_act * sigmoid_pre * (1.0 + pre_act * (1.0 - sigmoid_pre))
    grad_down = grad_scale * jnp.einsum("rfc,rfkd->fkcd", activation, cot_sel, precision=highest)
    back_terms = jnp.einsum("rfc,fkdc->rfkd", grad_pre, up_full, precision=highest)
    onehot = (
        up_index[:, :, None] == jnp.arange(block_count, dtype=jnp.int32)[None, None, :]
    ).astype(jnp.float32)
    partial_value = jnp.einsum("rfkd,fkj->rjd", back_terms, onehot, precision=highest).reshape(
        row_count, -1
    )
    grad_up = grad_scale * jnp.einsum("rfkd,rfc->fkdc", x_sel, grad_pre, precision=highest)
    input_grad = lax.psum_scatter(partial_value, "hid", scatter_dimension=1, tiled=True)
    up_share, down_share = (
        lax.psum_scatter(grad_up, "tok", scatter_dimension=2, tiled=True),
        lax.psum_scatter(grad_down, "tok", scatter_dimension=2, tiled=True),
    )
    return (input_grad, 0.9 * mom_up + up_share, 0.9 * mom_down + down_share)


def solution(mesh):
    return jax.shard_map(
        shards,
        mesh=mesh,
        in_specs=(
            P("tok", None),
            P("tok", None),
            P("hid", None, "tok", None),
            P("hid", None, "tok", None),
            P("hid", None),
            P("hid", None),
            P("hid", None, "tok", None),
            P("hid", None, "tok", None),
        ),
        out_specs=(P("tok", "hid"), P("hid", None, "tok", None), P("hid", None, "tok", None)),
        check_vma=False,
    )
```

profile of v0, /device:TPU:2, one launch (start us, length us, event | category | flops | bytes accessed | tf_op | source)
XLA Modules:
  0.0 435.1 jit_solution(1202382156357738444)
XLA Ops:
  7.2 1.6 copy.59
  8.9 1.6 copy.51
  10.5 3.0 copy.47
  13.5 1.9 copy.49
  15.6 2.7 gather_fusion
  18.3 5.3 %copy.50 = f32[14,4,128,128]{2,3,1,0:T(8,128)} copy(f32[14,4,128,128]{3,2,1,0:T(8,128)} %bitcast.75) | data formatting | bytes 7340032 | tf_op jit(solution)/shard_map/jit(_take)/gather | solution.py:20
  23.7 1.9 copy.55
  25.6 1.9 copy.57
  27.8 2.7 gather_fusion.1
  30.4 5.1 %copy.58 = f32[14,4,128,128]{2,3,1,0:T(8,128)} copy(f32[14,4,128,128]{3,2,1,0:T(8,128)} %bitcast.76) | data formatting | bytes 7340032 | tf_op jit(solution)/shard_map/jit(_take)/gather | solution.py:19
  35.7 57.8 %all-gather.5.cloned.1.call-done = f32[14,4,128,128]{3,1,0,2:T(4,128)} async-done(((f32[14,4,4,128]{3,1,0,2:T(4,128)}), f32[14,4,128,128]{3,1,0,2:T(4,128)}) %all-gather.5.cloned.1.call-update) | async-done | bytes 3670032 | tf_op jit(solution)/shard_map/all_gather | solution.py:13
  93.5 9.6 %fusion.39 = f32[128,14,128]{2,0,1:T(8,128)S(1)} fusion(f32[14,4,128,128]{3,1,0,2:T(4,128)} %all-gather.5.cloned.1.call-done, f32[14,4,128,128]{2,3,1,0:T(8,128)} %copy.58, pred[14,4]{1,0:T(8,128)(4,1)S(1)} %copy.54), kind=kOutput, calls=%fused_computation.33 | convolution fusion | flops 1410203648 | bytes 8257592 | tf_op jit(solution)/shard_map/rfkd,fkdc->rfc/dot_general | solution.py:21
  103.1 5.5 %multiply_bitcast_fusion = f32[14,4,128,128]{2,3,1,0:T(8,128)} fusion(f32[14,4,128,128]{2,3,1,0:T(8,128)S(1)} %copy-done, pred[14,4]{1,0:T(8,128)(4,1)S(1)} %copy.46, f32[128,14,128]{2,0,1:T(8,128)S(1)} %fusion.39), kind=kOutput, calls=%fused_computation.13 | convolution fusion | flops 1412038656 | bytes 8257592 | tf_op jit(solution)/shard_map/rfc,rfkd->fkcd/dot_general | solution.py:26
  108.6 65.5 %all-gather.3.cloned.1.call-done = f32[14,4,128,128]{3,1,0,2:T(4,128)} async-done(((f32[14,4,4,128]{3,1,0,2:T(4,128)}), f32[14,4,128,128]{3,1,0,2:T(4,128)}) %all-gather.3.cloned.1.call-update) | async-done | bytes 3670032 | tf_op jit(solution)/shard_map/all_gather | solution.py:14
  174.0 9.8 %fusion.54 = f32[128,14,128,1]{2,0,3,1:T(8,128)S(1)} fusion(f32[14,4,128,128]{3,1,0,2:T(4,128)} %all-gather.3.cloned.1.call-done, f32[14,4,128,128]{2,3,1,0:T(8,128)} %copy.50, pred[14,4]{1,0:T(8,128)(4,1)S(1)} %copy.46, f32[128,14,128]{2,0,1:T(8,128)S(1)} %fusion.39), kind=kOutput, calls=%fused_computation.36 | convolution fusion | flops 1412038656 | bytes 9175096 | tf_op jit(solution)/shard_map/rfkd,fkcd->rfc/dot_general | solution.py:24
  183.8 5.3 %fusion.20 = f32[14,4,128,128]{3,2,1,0:T(8,128)} fusion(f32[128,14,128,1]{2,0,3,1:T(8,128)S(1)} %fusion.54, f32[14,4,128,128]{2,3,1,0:T(8,128)S(1)} %copy-done.1, pred[14,4]{1,0:T(8,128)(4,1)S(1)} %copy.54), kind=kOutput, calls=%fused_computation.22 | convolution fusion | flops 1411121152 | bytes 8257592 | tf_op jit(solution)/shard_map/rfkd,rfc->fkdc/dot_general | solution.py:34
  189.1 5.1 %copy.64 = f32[14,4,128,128]{3,2,1,0:T(8,128)} copy(f32[14,4,128,128]{2,3,1,0:T(8,128)} %multiply_bitcast_fusion) | data formatting | bytes 7340032 | tf_op jit(solution)/shard_map/mul | solution.py:26
  194.6 6.0 %fusion.23 = f32[128,14,4,128]{3,0,2,1:T(8,128)S(1)} fusion(f32[128,14,128,1]{2,0,3,1:T(8,128)S(1)} %fusion.54, f32[14,4,128,128]{3,1,0,2:T(4,128)} %all-gather.5.cloned.1.call-done), kind=kOutput, calls=%fused_computation.23 | convolution fusion | flops 1409286144 | bytes 8257536 | tf_op jit(solution)/shard_map/rfc,fkdc->rfkd/dot_general | solution.py:27
  200.6 3.9 fusion
  204.5 3.0 copy.98
  207.5 0.6 dynamic-slice
  208.7 181.7 %all-reduce.5.cloned.1.call-done = (f32[14,4,128,128]{3,2,1,0:T(8,128)}, f32[14,4,128,128]{3,2,1,0:T(8,128)}) async-done(((f32[14,4,128,128]{3,2,1,0:T(8,128)}, f32[14,4,128,128]{3,2,1,0:T(8,128)}), (f32[14,4,128,128]{3,2,1,0:T(8,128)}, f32[14,4,128,128]{3,2,1,0:T(8,128)})) %all-reduce.5.cloned.1.call-update) | async-done | bytes 7340048
  390.5 1.8 dynamic-slice_add_fusion
  392.3 36.3 %reduce-scatter.4.cloned.1.call-done = f32[128,512]{1,0:T(8,128)} async-done(((f32[128,4096]{1,0:T(8,128)}), f32[128,512]{1,0:T(8,128)}) %reduce-scatter.4.cloned.1.call-update) | async-done | bytes 262160 | tf_op jit(solution)/shard_map/reduce_scatter | solution.py:35
  (36 shorter events, 1.2 us)
Async XLA Ops:
  7.2 86.3 %all-gather.5.cloned.1.call-start = ((), (), s32[]{:S(2)}) async-start(), calls=%async_computation.2 | async-start | bytes 3784704 | tf_op jit(solution)/shard_map/all_gather | solution.py:13
  8.8 165.2 %all-gather.3.cloned.1.call-start = ((), (), s32[]{:S(2)}) async-start(), calls=%async_computation.1 | async-start | bytes 3784704 | tf_op jit(solution)/shard_map/all_gather | solution.py:14
  10.5 5.0 %copy-start.6 = (s32[14,4]{0,1:T(4,128)S(1)}, s32[14,4]{0,1:T(4,128)}, u32[]{:S(2)}) copy-start(s32[14,4]{0,1:T(4,128)} %param.15) | copy-start | bytes 676
  10.5 380.0 %all-reduce.5.cloned.1.call-start = ((), (), s32[]{:S(2)}) async-start(), calls=%async_computation.4 | async-start | bytes 14680064
  18.3 5.4 %copy-start.2 = (f32[128,4096]{1,0:T(8,128)S(1)}, f32[128,4096]{1,0:T(8,128)}, u32[]{:S(2)}) copy-start(f32[128,4096]{1,0:T(8,128)} %param.10) | copy-start | bytes 6291460
  23.7 3.9 copy-start.5
  93.5 9.7 %copy-start = (f32[14,4,128,128]{2,3,1,0:T(8,128)S(1)}, f32[14,4,128,128]{2,3,1,0:T(8,128)}, u32[]{:S(2)}) copy-start(f32[14,4,128,128]{2,3,1,0:T(8,128)} %copy.50) | copy-start | bytes 11010052
  174.0 9.8 %copy-start.1 = (f32[14,4,128,128]{2,3,1,0:T(8,128)S(1)}, f32[14,4,128,128]{2,3,1,0:T(8,128)}, u32[]{:S(2)}) copy-start(f32[14,4,128,128]{2,3,1,0:T(8,128)} %copy.58) | copy-start | bytes 11010052
  194.3 234.3 %reduce-scatter.4.cloned.1.call-start = ((), (), s32[]{:S(2)}) async-start(), calls=%async_computation.3 | async-start | bytes 2359296 | tf_op jit(solution)/shard_map/reduce_scatter | solution.py:35
  204.4 3.1 copy-start.7
  204.5 186.0 %copy-start.3 = (f32[14,4,4,128]{3,2,1,0:T(4,128)S(1)}, f32[14,4,4,128]{3,2,1,0:T(4,128)}, u32[]{:S(2)}) copy-start(f32[14,4,4,128]{3,2,1,0:T(4,128)} %param.17) | copy-start | bytes 344068
  204.5 186.0 %copy-start.4 = (f32[14,4,4,128]{3,2,1,0:T(4,128)S(1)}, f32[14,4,4,128]{3,2,1,0:T(4,128)}, u32[]{:S(2)}) copy-start(f32[14,4,4,128]{3,2,1,0:T(4,128)} %param.16) | copy-start | bytes 344068
Sparse Core Ops, SparseCore 0:
  11.1 82.2 all-gather.4
  96.6 77.4 all-gather.2
  194.4 196.0 all-reduce.4
  393.5 35.0 reduce-scatter.3
where the time goes:
time: 436 us; the launch traced here: 435 us
  waiting for transfers between devices  341 us (78%)
  matrix products  40 us (9%)
  local copies, waits for them, and re-layouts  36.9 us (8%)
  between operations  14.6 us (3%)
    unnamed x5, waiting for transfers between devices  182 us
    all_gather x1, waiting for transfers between devices, shards(): lax.all_gather(down_blocks, 'tok', axis=2, tiled=True)  65.5 us
    all_gather x1, waiting for transfers between devices, shards(): lax.all_gather(up_blocks, 'tok', axis=2, tiled=True)  57.8 us
    reduce_scatter x1, waiting for transfers between devices, shards(): lax.psum_scatter(partial_value, 'hid', scatter_dimension=1, tiled=True)  36.3 us
    unnamed x22, local copies, waits for them, and re-layouts  11.6 us
    dot_general x1, matrix products, shards(): jnp.einsum('rfkd,fkcd->rfc', cot_sel, down_full, precision=highest)  9.77 us
    dot_general x1, matrix products, shards(): pre_act = jnp.einsum('rfkd,fkdc->rfc', x_sel, up_full, precision=highest)  9.65 us
  transfers between devices with their start and end apart: 4, of which 4 were waited for; matrix products, arithmetic and copies ran while one was open for 13% of the time, Pallas kernels for 0%

commit v1 on v0

--- a/solution.py
+++ b/solution.py
@@ -11,7 +11,9 @@
     block_count = inputs.shape[1] // block
     up_full, down_full = (
         lax.all_gather(up_blocks, "tok", axis=2, tiled=True),
-        lax.all_gather(down_blocks, "tok", axis=2, tiled=True),
+        jnp.concatenate(
+            lax.all_to_all(jnp.stack([down_blocks] * lax.axis_size("tok")), "tok", 0, 0), axis=2
+        ),
     )
     grad_scale = (row_count * lax.axis_size("tok")) ** (-0.5)
     x_blocks = inputs.reshape(row_count, block_count, block)

time: 436 us -> 405 us (0.929)
  waiting for transfers between devices: 341 us -> 298 us
  starting transfers between devices: 0.42 us -> 12.2 us
  local copies, waits for them, and re-layouts: 36.9 us -> 41.8 us
    all_to_all x0 -> x1, waiting for transfers between devices: none -> 73.6 us  [shards(): lax.all_to_all(jnp.stack([down_blocks] * lax.axis_size('tok')), 'tok', 0, 0)]
    all_gather x1 -> x0, waiting for transfers between devices: 65.5 us -> none  [shards(): lax.all_gather(down_blocks, 'tok', axis=2, tiled=True)]
    all_gather x1, waiting for transfers between devices: 57.8 us -> 5.07 us  [shards(): lax.all_gather(up_blocks, 'tok', axis=2, tiled=True)]
    all_to_all x0 -> x1, starting transfers between devices: none -> 11.8 us  [shards(): lax.all_to_all(jnp.stack([down_blocks] * lax.axis_size('tok')), 'tok', 0, 0)]
    reshape x0 -> x1, local copies, waits for them, and re-layouts: none -> 5.03 us  [shards(): jnp.concatenate(lax.all_to_all(jnp.stack([down_blocks] * lax.axis_size('t...]
    unnamed x22 -> x27, local copies, waits for them, and re-layouts: 11.6 us -> 8.02 us
    unnamed x5 -> x4, waiting for transfers between devices: 182 us -> 183 us
  transfers between devices with their start and end apart: 4 -> 4, of which waited for: 4 -> 4; matrix products, arithmetic and copies ran while one was open for 13% -> 11% of each run, Pallas kernels for 0% -> 0%
where the time goes in v1:
time: 405 us
  waiting for transfers between devices  298 us (74%)
  local copies, waits for them, and re-layouts  41.8 us (10%)
  matrix products  36.7 us (9%)
  between operations  14.6 us (4%)
  starting transfers between devices  12.2 us (3%)
    unnamed x4, waiting for transfers between devices  183 us
    all_to_all x1, waiting for transfers between devices, shards(): lax.all_to_all(jnp.stack([down_blocks] * lax.axis_size('tok')), 'tok', 0, 0)  73.6 us
    reduce_scatter x1, waiting for transfers between devices, shards(): lax.psum_scatter(partial_value, 'hid', scatter_dimension=1, tiled=True)  36.4 us
    all_to_all x1, starting transfers between devices, shards(): lax.all_to_all(jnp.stack([down_blocks] * lax.axis_size('tok')), 'tok', 0, 0)  11.8 us
    dot_general x1, matrix products, shards(): pre_act = jnp.einsum('rfkd,fkdc->rfc', x_sel, up_full, precision=highest)  9.74 us
  transfers between devices with their start and end apart: 4, of which 4 were waited for; matrix products, arithmetic and copies ran while one was open for 11% of the time, Pallas kernels for 0%

profile of v1, /device:TPU:2, one launch (start us, length us, event | category | flops | bytes accessed | tf_op | source)
XLA Modules:
  0.0 404.8 jit_solution(17248044049763401300)
XLA Ops:
  7.2 3.6 stack.2
  10.8 11.8 %all-to-all-start = ((f32[32,14,4,4,128]{4,3,2,1,0:T(4,128)}), f32[32,14,4,4,128]{4,3,2,1,0:T(4,128)}, u32[]{:S(2)}, u32[]{:S(2)}) async-start(f32[32,14,4,4,128]{4,3,2,1,0:T(4,128)} %stack.2), calls=%async_computation | async-start | bytes 7340032 | tf_op jit(solution)/shard_map/all_to_all | solution.py:15
  23.4 1.9 copy.47
  25.4 1.9 copy.49
  27.5 2.6 gather_fusion
  30.1 5.3 %copy.50 = f32[14,4,128,128]{2,3,1,0:T(8,128)} copy(f32[14,4,128,128]{3,2,1,0:T(8,128)} %bitcast.79) | data formatting | bytes 7340032 | tf_op jit(solution)/shard_map/jit(_take)/gather | solution.py:22
  35.5 1.8 copy.54
  37.3 1.9 copy.56
  39.4 2.6 gather_fusion.1
  42.1 5.1 %copy.57 = f32[14,4,128,128]{2,3,1,0:T(8,128)} copy(f32[14,4,128,128]{3,2,1,0:T(8,128)} %bitcast.80) | data formatting | bytes 7340032 | tf_op jit(solution)/shard_map/jit(_take)/gather | solution.py:21
  47.3 73.6 %all-to-all-done = f32[32,14,4,4,128]{4,3,2,1,0:T(4,128)} async-done(((f32[32,14,4,4,128]{4,3,2,1,0:T(4,128)}), f32[32,14,4,4,128]{4,3,2,1,0:T(4,128)}, u32[]{:S(2)}, u32[]{:S(2)}) %all-to-all-start) | async-done | bytes 3670048 | tf_op jit(solution)/shard_map/all_to_all | solution.py:15
  120.9 5.0 %copy.51 = f32[14,4,32,4,128]{4,3,2,1,0:T(4,128)} copy(f32[14,4,32,4,128]{4,3,1,0,2:T(4,128)} %bitcast.4) | data formatting | bytes 7340032 | tf_op jit(solution)/shard_map/reshape | solution.py:14
  125.9 5.1 %all-gather.2.cloned.1.call-done = f32[14,4,128,128]{3,1,0,2:T(4,128)} async-done(((f32[14,4,4,128]{3,1,0,2:T(4,128)}), f32[14,4,128,128]{3,1,0,2:T(4,128)}) %all-gather.2.cloned.1.call-update) | async-done | bytes 3670032 | tf_op jit(solution)/shard_map/all_gather | solution.py:13
  131.0 9.7 %fusion.36 = f32[128,14,128]{2,0,1:T(8,128)S(1)} fusion(f32[14,4,128,128]{3,1,0,2:T(4,128)} %all-gather.2.cloned.1.call-done, f32[14,4,128,128]{2,3,1,0:T(8,128)} %copy.57, pred[14,4]{1,0:T(8,128)(4,1)S(1)} %copy.53), kind=kOutput, calls=%fused_computation.32 | convolution fusion | flops 1410203648 | bytes 8257592 | tf_op jit(solution)/shard_map/rfkd,fkdc->rfc/dot_general | solution.py:23
  140.8 5.5 %multiply_bitcast_fusion = f32[14,4,128,128]{2,3,1,0:T(8,128)} fusion(f32[14,4,128,128]{2,3,1,0:T(8,128)S(1)} %copy-done, pred[14,4]{1,0:T(8,128)(4,1)S(1)} %copy.46, f32[128,14,128]{2,0,1:T(8,128)S(1)} %fusion.36), kind=kOutput, calls=%fused_computation.12 | convolution fusion | flops 1412038656 | bytes 8257592 | tf_op jit(solution)/shard_map/rfc,rfkd->fkcd/dot_general | solution.py:28
  146.2 6.3 %fusion.47 = f32[128,14,128,1]{2,0,3,1:T(8,128)S(1)} fusion(f32[14,4,128,128]{3,2,1,0:T(8,128)S(1)} %bitcast.78, f32[14,4,128,128]{2,3,1,0:T(8,128)S(1)} %copy-done, pred[14,4]{1,0:T(8,128)(4,1)S(1)} %copy.46, f32[128,14,128]{2,0,1:T(8,128)S(1)} %fusion.36), kind=kOutput, calls=%fused_computation.35 | convolution fusion | flops 1412038656 | bytes 9175096 | tf_op jit(solution)/shard_map/rfkd,fkcd->rfc/dot_general | solution.py:26
  152.6 5.3 %fusion.19 = f32[14,4,128,128]{3,2,1,0:T(8,128)} fusion(f32[128,14,128,1]{2,0,3,1:T(8,128)S(1)} %fusion.47, f32[14,4,128,128]{2,3,1,0:T(8,128)S(1)} %copy-done.1, pred[14,4]{1,0:T(8,128)(4,1)S(1)} %copy.53), kind=kOutput, calls=%fused_computation.21 | convolution fusion | flops 1411121152 | bytes 8257592 | tf_op jit(solution)/shard_map/rfkd,rfc->fkdc/dot_general | solution.py:36
  157.9 5.1 %copy.63 = f32[14,4,128,128]{3,2,1,0:T(8,128)} copy(f32[14,4,128,128]{2,3,1,0:T(8,128)} %multiply_bitcast_fusion) | data formatting | bytes 7340032 | tf_op jit(solution)/shard_map/mul | solution.py:28
  163.3 6.0 %fusion.22 = f32[128,14,4,128]{3,0,2,1:T(8,128)S(1)} fusion(f32[128,14,128,1]{2,0,3,1:T(8,128)S(1)} %fusion.47, f32[14,4,128,128]{3,1,0,2:T(4,128)} %all-gather.2.cloned.1.call-done), kind=kOutput, calls=%fused_computation.22 | convolution fusion | flops 1409286144 | bytes 8257536 | tf_op jit(solution)/shard_map/rfc,fkdc->rfkd/dot_general | solution.py:29
  169.3 3.9 fusion
  173.2 3.0 copy.87
  177.5 182.5 %all-reduce.5.cloned.1.call-done = (f32[14,4,128,128]{3,2,1,0:T(8,128)}, f32[14,4,128,128]{3,2,1,0:T(8,128)}) async-done(((f32[14,4,128,128]{3,2,1,0:T(8,128)}, f32[14,4,128,128]{3,2,1,0:T(8,128)}), (f32[14,4,128,128]{3,2,1,0:T(8,128)}, f32[14,4,128,128]{3,2,1,0:T(8,128)})) %all-reduce.5.cloned.1.call-update) | async-done | bytes 7340048
  360.0 1.8 dynamic-slice_add_fusion
  361.8 36.4 %reduce-scatter.4.cloned.1.call-done = f32[128,512]{1,0:T(8,128)} async-done(((f32[128,4096]{1,0:T(8,128)}), f32[128,512]{1,0:T(8,128)}) %reduce-scatter.4.cloned.1.call-update) | async-done | bytes 262160 | tf_op jit(solution)/shard_map/reduce_scatter | solution.py:37
  (42 shorter events, 2.4 us)
Async XLA Ops:
  10.8 11.9 %copy-start.7 = (f32[14,4,4,128]{3,2,1,0:T(4,128)S(1)}, f32[14,4,4,128]{3,2,1,0:T(4,128)}, u32[]{:S(2)}) copy-start(f32[14,4,4,128]{3,2,1,0:T(4,128)} %param.12) | copy-start | bytes 344068
  10.8 12.6 %copy-start.3 = (f32[128,4096]{1,0:T(8,128)S(1)}, f32[128,4096]{1,0:T(8,128)}, u32[]{:S(2)}) copy-start(f32[128,4096]{1,0:T(8,128)} %param.11) | copy-start | bytes 6291460
  10.8 110.1 %all-to-all-start = ((f32[32,14,4,4,128]{4,3,2,1,0:T(4,128)}), f32[32,14,4,4,128]{4,3,2,1,0:T(4,128)}, u32[]{:S(2)}, u32[]{:S(2)}) async-start(f32[32,14,4,4,128]{4,3,2,1,0:T(4,128)} %stack.2), calls=%async_computation | async-start | bytes 7340032 | tf_op jit(solution)/shard_map/all_to_all | solution.py:15
  22.6 108.4 %all-gather.2.cloned.1.call-start = ((), (), s32[]{:S(2)}) async-start(), calls=%async_computation.2 | async-start | bytes 3784704 | tf_op jit(solution)/shard_map/all_gather | solution.py:13
  23.4 3.9 copy-start.9
  23.4 336.6 %all-reduce.5.cloned.1.call-start = ((), (), s32[]{:S(2)}) async-start(), calls=%async_computation.4 | async-start | bytes 14680064
  30.1 5.4 %copy-start.4 = (f32[128,4096]{1,0:T(8,128)S(1)}, f32[128,4096]{1,0:T(8,128)}, u32[]{:S(2)}) copy-start(f32[128,4096]{1,0:T(8,128)} %param.10) | copy-start | bytes 6291460
  35.5 3.7 copy-start.8
  131.0 9.8 %copy-start = (f32[14,4,128,128]{2,3,1,0:T(8,128)S(1)}, f32[14,4,128,128]{2,3,1,0:T(8,128)}, u32[]{:S(2)}) copy-start(f32[14,4,128,128]{2,3,1,0:T(8,128)} %copy.50) | copy-start | bytes 11010052
  140.7 5.5 %copy-start.2 = (f32[14,4,32,4,128]{4,3,2,1,0:T(4,128)S(1)}, f32[14,4,32,4,128]{4,3,2,1,0:T(4,128)}, u32[]{:S(2)}) copy-start(f32[14,4,32,4,128]{4,3,2,1,0:T(4,128)} %copy.51) | copy-start | bytes 11010052
  146.2 6.3 %copy-start.1 = (f32[14,4,128,128]{2,3,1,0:T(8,128)S(1)}, f32[14,4,128,128]{2,3,1,0:T(8,128)}, u32[]{:S(2)}) copy-start(f32[14,4,128,128]{2,3,1,0:T(8,128)} %copy.57) | copy-start | bytes 11010052
  163.0 235.2 %reduce-scatter.4.cloned.1.call-start = ((), (), s32[]{:S(2)}) async-start(), calls=%async_computation.3 | async-start | bytes 2359296 | tf_op jit(solution)/shard_map/reduce_scatter | solution.py:37
  173.2 3.1 copy-start.10
  173.2 186.8 %copy-start.5 = (f32[14,4,4,128]{3,2,1,0:T(4,128)S(1)}, f32[14,4,4,128]{3,2,1,0:T(4,128)}, u32[]{:S(2)}) copy-start(f32[14,4,4,128]{3,2,1,0:T(4,128)} %param.17) | copy-start | bytes 344068
  173.2 186.8 %copy-start.6 = (f32[14,4,4,128]{3,2,1,0:T(4,128)S(1)}, f32[14,4,4,128]{3,2,1,0:T(4,128)}, u32[]{:S(2)}) copy-start(f32[14,4,4,128]{3,2,1,0:T(4,128)} %param.16) | copy-start | bytes 344068
Sparse Core Ops, SparseCore 0:
  26.6 104.3 all-gather.1
  163.1 196.7 all-reduce.4
  363.1 35.0 reduce-scatter.3
